TPU v7x, 256 devices: a whole 4x4x8 slice. The times are simulated.
256 devices in a mesh: frame: 8 (over z), tile: 32 (over x, y, core).
Axes of the slice: x: 4, y: 4, z: 8, core: 2. Of those that a mesh axis runs over, the one named last changes fastest.
Arguments:
- displacement: bfloat16 [512, 2, 32, 4096], P('frame', None, 'tile'), may hold values from -256 to 256
Outputs:
- basis: bfloat16 [512, 3, 32, 4096], P(None, None, 'tile', 'frame')
- factor: float32 [512, 512], replicated
All inputs are finite; a program needn't handle non-finite values.
Results may differ from a plain program's by a relative error of at most 0.0053.
The roundings to bfloat16 on the way count: a program that leaves them out, or rounds other values in their place, can miss the bound.
Values may be sent and summed in bfloat16 or wider, within the bound.
No kernel may reach another device: no remote copies, remote signals or barrier semaphores. Data moves between devices by JAX's collectives and lax.ppermute only.
A program may use at most 64 MiB of HBM per device.

v0:
```python
import math
import jax
import jax.numpy as jnp
from jax import lax
from jax.sharding import PartitionSpec as P


def with_halo(array, sides, width):
    for axis, dim in sides:
        peers, length = (lax.axis_size(axis), array.shape[dim])
        up = [(i, (i + 1) % peers) for i in range(peers - 1)]
        down = [(j, i) for i, j in up]
        last = lax.slice_in_dim(array, length - width, length, axis=dim)
        first = lax.slice_in_dim(array, 0, width, axis=dim)
        before = lax.ppermute(last, axis, up)
        after = lax.ppermute(first, axis, down)
        array = jnp.concatenate([before, array, after], axis=dim)
    return array


def derivative(center, before, after, first, final):
    return jnp.where(
        first, after - center, jnp.where(final, center - before, (after - before) * 0.5)
    )


def column_derivative(center):
    width = center.shape[-1]
    after = jnp.concatenate([center[..., 1:], center[..., -1:]], axis=-1)
    before = jnp.concatenate([center[..., :1], center[..., :-1]], axis=-1)
    column = jnp.arange(width, dtype=jnp.int32)
    return derivative(center, before, after, column == 0, column == width - 1)


def combine_strain(d_rows, d_cols):
    return jnp.stack(
        [d_cols[:, 0], d_rows[:, 1], 0.5 * (d_rows[:, 0] + d_cols[:, 1])], axis=1
    ).astype(jnp.bfloat16)


def local(displacement):
    rows = displacement.shape[2]
    full_width = displacement.shape[3]
    total_rows = lax.axis_size("tile") * rows
    scale = math.sqrt(3 * total_rows * full_width)
    row_global = lax.axis_index("tile") * rows + jnp.arange(rows, dtype=jnp.int32)
    first = (row_global == 0)[:, None]
    final = (row_global == total_rows - 1)[:, None]
    padded = with_halo(displacement, (("tile", 2),), 1)
    field = padded.astype(jnp.float32)
    center = field[:, :, 1:-1, :]
    d_rows = derivative(center, field[:, :, :-2, :], field[:, :, 2:, :], first, final)
    d_cols = column_derivative(center)
    strain = combine_strain(d_rows, d_cols)
    pixel_major = lax.all_to_all(strain, "frame", split_axis=3, concat_axis=0, tiled=True)
    frames = pixel_major.shape[0]
    snapshot_half = pixel_major.reshape(frames, -1)
    local_gram = lax.dot_general(
        snapshot_half, snapshot_half, (((1,), (1,)), ((), ())), preferred_element_type=jnp.float32
    )
    gram = lax.psum(local_gram, ("frame", "tile"))
    lower = jnp.linalg.cholesky(gram)
    snapshot = snapshot_half.astype(jnp.float32)
    solved = lax.linalg.triangular_solve(lower, snapshot, left_side=True, lower=True)
    basis = (solved * scale).astype(jnp.bfloat16).reshape(pixel_major.shape)
    return (basis, lower.T / scale)


def solution(mesh):
    return jax.shard_map(
        local,
        mesh=mesh,
        in_specs=(P("frame", None, "tile", None),),
        out_specs=(P(None, None, "tile", "frame"), P()),
        check_vma=False,
    )
```

profile of v0, /device:TPU:2, one launch (start us, length us, event | category | flops | bytes accessed | tf_op | source)
XLA Modules:
  0.0 526.9 jit_solution(18431249091505621572)
XLA Ops:
  7.2 1.8 copy.46
  9.0 1.9 collective-permute-start
  10.9 5.8 %collective-permute-start.1 = (bf16[64,2,1,4096]{3,0,2,1:T(8,128)(2,1)S(1)}, bf16[64,2,1,4096]{3,0,2,1:T(8,128)(2,1)S(1)}, u32[]{:S(2)}, u32[]{:S(2)}) collective-permute-start(bf16[64,2,1,4096]{3,0,2,1:T(8,128)(2,1)S(1)} %copy.46), channel_id=1, source_target_pairs={{1,0},{2,1},{3,2},{4,3},{5,4},{6,5},{7,6},{8,7},{9,8},{10,9},{11,1... | collective-permute-start | bytes 3145736 | tf_op jit(solution)/shard_map/ppermute | solution.py:16
  16.7 10.5 %collective-permute-done = bf16[64,2,1,4096]{3,0,2,1:T(8,128)(2,1)S(1)} collective-permute-done((bf16[64,2,1,4096]{3,0,2,1:T(8,128)(2,1)S(1)}, bf16[64,2,1,4096]{3,0,2,1:T(8,128)(2,1)S(1)}, u32[]{:S(2)}, u32[]{:S(2)}) %collective-permute-start) | collective-permute-done | bytes 1048608 | tf_op jit(solution)/shard_map/ppermute | solution.py:15
  27.2 1.8 collective-permute-done.1
  29.0 0.5 maximum_convert_fusion
  29.5 0.7 fusion.35
  30.3 1.5 select_select_fusion
  32.2 4.7 copy.49
  36.9 6.1 %reshape.243 = bf16[8,2,49152]{2,1,0:T(2,128)(2,1)S(1)} reshape(bf16[4096,1,3,64]{3,2,1,0:T(4,128)(2,1)} %bitcast.77) | data formatting | bytes 3145728
  43.0 48.1 %all_to_all.15 = bf16[8,2,49152]{2,1,0:T(2,128)(2,1)S(1)} all-to-all(bf16[8,2,49152]{2,1,0:T(2,128)(2,1)S(1)} %reshape.243), channel_id=1, replica_groups=mesh['frame'=8,'tile'=32] {'frame'}, dimensions={0} | all-to-all | bytes 3145728 | tf_op jit(solution)/shard_map/all_to_all | solution.py:55
  91.2 4.8 reshape.244
  96.0 4.8 copy.67
  100.8 1.4 copy.51
  102.1 0.5 copy.69
  102.7 2.0 fusion.36
  104.9 2.1 convert_element_type.26
  107.0 0.3 copy.54
  107.3 0.8 copy.70
  108.2 248.2 %all-reduce.3.cloned.1.call-done = f32[512,512]{0,1:T(8,128)} async-done(((f32[512,512]{0,1:T(8,128)}), f32[512,512]{0,1:T(8,128)}) %all-reduce.3.cloned.1.call-update) | async-done | bytes 1048592 | tf_op jit(solution)/shard_map/psum | solution.py:61
  356.4 1.6 copy.53
  358.3 11.7 %cholesky.104 = f32[128,128]{1,0:T(8,128)S(1)} custom-call(f32[128,128]{1,0:T(8,128)S(1)} %cholesky.266), custom_call_target="Cholesky" | custom-call | tf_op jit(solution)/shard_map/jit(cholesky)/cholesky | solution.py:62
  370.2 9.8 %custom-call.30 = f32[1,128,128]{1,2,0:T(8,128)S(1)} custom-call(f32[1,128,128]{2,1,0:T(8,128)S(1)} %get-tuple-element.45), custom_call_target="InvertDiagBlocksLowerTriangular" | custom-call | tf_op jit(solution)/shard_map/jit(cholesky)/cholesky | solution.py:62
  380.0 0.3 constant_dynamic-update-slice_fusion.3
  380.4 0.3 convolution_subtract_fusion.3
  380.7 11.8 %cholesky.217 = f32[128,128]{1,0:T(8,128)S(1)} custom-call(f32[128,128]{1,0:T(8,128)S(1)} %cholesky.270), custom_call_target="Cholesky" | custom-call | tf_op jit(solution)/shard_map/jit(cholesky)/cholesky | solution.py:62
  392.6 0.6 compare_reduce_fusion.2
  393.2 0.6 compare_reduce_fusion.3
  393.8 9.8 %custom-call.31 = f32[1,128,128]{1,2,0:T(8,128)S(1)} custom-call(f32[1,128,128]{2,1,0:T(8,128)S(1)} %get-tuple-element.42), custom_call_target="InvertDiagBlocksLowerTriangular" | custom-call | tf_op jit(solution)/shard_map/jit(cholesky)/cholesky | solution.py:62
  403.6 0.3 convolution_dynamic-update-slice_fusion
  403.9 0.4 convolution_subtract_fusion.4
  404.3 11.7 %cholesky.238 = f32[128,128]{1,0:T(8,128)S(1)} custom-call(f32[128,128]{1,0:T(8,128)S(1)} %cholesky.275), custom_call_target="Cholesky" | custom-call | tf_op jit(solution)/shard_map/jit(cholesky)/cholesky | solution.py:62
  416.1 0.7 compare_reduce_fusion.1
  416.7 9.8 %custom-call.32 = f32[1,128,128]{1,2,0:T(8,128)S(1)} custom-call(f32[1,128,128]{2,1,0:T(8,128)S(1)} %get-tuple-element.39), custom_call_target="InvertDiagBlocksLowerTriangular" | custom-call | tf_op jit(solution)/shard_map/jit(cholesky)/cholesky | solution.py:62
  426.7 0.4 convolution_subtract_fusion.5
  427.1 11.9 %cholesky.255 = f32[128,128]{1,0:T(8,128)S(1)} custom-call(f32[128,128]{1,0:T(8,128)S(1)} %convolution_subtract_fusion.5), custom_call_target="Cholesky" | custom-call | tf_op jit(solution)/shard_map/jit(cholesky)/cholesky | solution.py:62
  439.1 0.7 compare_reduce_fusion
  442.3 0.3 multiply_bitcast_fusion
  442.6 10.0 %while.1 = (s32[]{:T(128)}, f32[512,512]{1,0:T(8,128)S(1)}, s32[4,2]{0,1:T(2,128)S(1)}, f32[4,128,128]{2,1,0:T(8,128)}, s32[]{:T(128)}) while((s32[]{:T(128)}, f32[512,512]{1,0:T(8,128)S(1)}, s32[4,2]{0,1:T(2,128)S(1)}, f32[4,128,128]{2,1,0:T(8,128)}, s32[]{:T(128)}) %tuple.39), condition=%wide.while_cond, body=%wide.while_body.sunk | while | flops 2 | bytes 132705 | solution.py:64
  442.7 0.5 fusion.46
  443.2 1.9 bitcast_dynamic-update-slice_fusion.2
  445.2 0.5 fusion.46
  445.7 1.9 bitcast_dynamic-update-slice_fusion.2
  447.7 0.5 fusion.46
  448.2 1.9 bitcast_dynamic-update-slice_fusion.2
  450.2 0.5 fusion.46
  450.7 1.9 bitcast_dynamic-update-slice_fusion.2
  452.6 40.2 %custom-call.33 = f32[4,128,128]{1,2,0:T(8,128)S(1)} custom-call(f32[4,128,128]{2,1,0:T(8,128)} %get-tuple-element.9), custom_call_target="InvertDiagBlocksLowerTriangular" | custom-call | tf_op jit(solution)/shard_map/triangular_solve | solution.py:64
  492.8 1.6 fusion.26
  494.4 2.1 convolution_subtract_fusion.2
  496.5 1.7 fusion.25
  498.3 1.9 convolution_subtract_fusion
  500.2 1.7 fusion.23
  501.9 3.4 fusion.1
  505.3 1.1 copy.57
  506.4 1.2 copy.56
  507.6 1.1 copy.55
  508.7 1.4 copy.58
  510.1 1.7 convolution_bitcast_fusion
  511.8 0.3 copy.62
  512.1 1.4 copy.61
  513.5 2.3 copy.60
  515.8 1.3 copy.64
  517.1 2.7 fusion.7
  (36 shorter events, 1.8 us)
Async XLA Ops:
  7.2 349.3 %all-reduce.3.cloned.1.call-start = ((), (), s32[]{:S(2)}) async-start(), calls=%async_computation.1 | async-start | bytes 2097152 | tf_op jit(solution)/shard_map/psum | solution.py:61
  9.0 18.2 %collective-permute-start = (bf16[64,2,1,4096]{3,0,2,1:T(8,128)(2,1)S(1)}, bf16[64,2,1,4096]{3,0,2,1:T(8,128)(2,1)S(1)}, u32[]{:S(2)}, u32[]{:S(2)}) collective-permute-start(bf16[64,2,1,4096]{3,0,2,1:T(8,128)(2,1)S(1)} %copy.46), channel_id=1, source_target_pairs={{0,1},{1,2},{2,3},{3,4},{4,5},{5,6},{6,7},{7,8},{8,9},{9,10},{10,1... | collective-permute-start | bytes 3145736 | tf_op jit(solution)/shard_map/ppermute | solution.py:15
  10.9 18.1 %collective-permute-start.1 = (bf16[64,2,1,4096]{3,0,2,1:T(8,128)(2,1)S(1)}, bf16[64,2,1,4096]{3,0,2,1:T(8,128)(2,1)S(1)}, u32[]{:S(2)}, u32[]{:S(2)}) collective-permute-start(bf16[64,2,1,4096]{3,0,2,1:T(8,128)(2,1)S(1)} %copy.46), channel_id=1, source_target_pairs={{1,0},{2,1},{3,2},{4,3},{5,4},{6,5},{7,6},{8,7},{9,8},{10,9},{11,1... | collective-permute-start | bytes 3145736 | tf_op jit(solution)/shard_map/ppermute | solution.py:16
  356.4 1.7 copy-start.1
  452.6 40.2 %copy-start.3 = (f32[512,512]{1,0:T(8,128)}, f32[512,512]{1,0:T(8,128)S(1)}, u32[]{:S(2)}) copy-start(f32[512,512]{1,0:T(8,128)S(1)} %get-tuple-element.100) | copy-start | bytes 3145732
  492.8 1.6 copy-start.4
  494.4 3.8 copy-start
  507.6 4.3 copy-start.2
Sparse Core Ops, SparseCore 0:
  104.8 251.5 all-reduce.2
where the time goes:
time: 532 us; the launch traced here: 527 us
  waiting for transfers between devices  261 us (49%)
  other arithmetic  127 us (24%)
  local copies, waits for them, and re-layouts  48.3 us (9%)
  blocking collectives  48.1 us (9%)
  matrix products  17.9 us (3%)
  between operations  17.2 us (3%)
  starting transfers between devices  7.71 us (1%)
    psum x1, waiting for transfers between devices, local(): gram = lax.psum(local_gram, ('frame', 'tile'))  248 us
    another operation x15, other arithmetic, local(): lower = jnp.linalg.cholesky(gram)  79.4 us
    all_to_all x1, blocking collectives, local(): lax.all_to_all(strain, 'frame', split_axis=3, concat_axis=0, tiled=True)  48.1 us
    another operation x2, other arithmetic, local(): lax.linalg.triangular_solve(lower, snapshot, left_side=True, lower=True)  40.2 us
    unnamed x16, local copies, waits for them, and re-layouts  15.4 us
    another operation x7, matrix products, local(): lax.linalg.triangular_solve(lower, snapshot, left_side=True, lower=True)  14.1 us
  transfers between devices with their start and end apart: 3, of which 3 were waited for; matrix products, arithmetic and copies ran while one was open for 1% of the time, Pallas kernels for 0%

commit v1 on v0

--- a/solution.py
+++ b/solution.py
@@ -58,7 +58,7 @@
     local_gram = lax.dot_general(
         snapshot_half, snapshot_half, (((1,), (1,)), ((), ())), preferred_element_type=jnp.float32
     )
-    gram = lax.psum(local_gram, ("frame", "tile"))
+    gram = lax.psum(lax.psum(local_gram, "frame"), "tile")
     lower = jnp.linalg.cholesky(gram)
     snapshot = snapshot_half.astype(jnp.float32)
     solved = lax.linalg.triangular_solve(lower, snapshot, left_side=True, lower=True)

time: 532 us -> 471 us (0.89)
  waiting for transfers between devices: 261 us -> 196 us
    psum x1 -> x2, waiting for transfers between devices: 248 us -> 184 us  [local(): gram = lax.psum(lax.psum(local_gram, 'frame'), 'tile')]
  transfers between devices with their start and end apart: 3 -> 4, of which waited for: 3 -> 4; matrix products, arithmetic and copies ran while one was open for 1% -> 1% of each run, Pallas kernels for 0% -> 0%
where the time goes in v1:
time: 471 us; the launch traced here: 462 us
  waiting for transfers between devices  196 us (42%)
  other arithmetic  127 us (27%)
  blocking collectives  48.1 us (10%)
  local copies, waits for them, and re-layouts  47.8 us (10%)
  matrix products  17.9 us (4%)
  between operations  17.2 us (4%)
  starting transfers between devices  8.22 us (2%)
    psum x2, waiting for transfers between devices, local(): gram = lax.psum(lax.psum(local_gram, 'frame'), 'tile')  184 us
    another operation x15, other arithmetic, local(): lower = jnp.linalg.cholesky(gram)  79.4 us
    all_to_all x1, blocking collectives, local(): lax.all_to_all(strain, 'frame', split_axis=3, concat_axis=0, tiled=True)  48.1 us
    another operation x2, other arithmetic, local(): lax.linalg.triangular_solve(lower, snapshot, left_side=True, lower=True)  40.2 us
    unnamed x16, local copies, waits for them, and re-layouts  15.4 us
    another operation x7, matrix products, local(): lax.linalg.triangular_solve(lower, snapshot, left_side=True, lower=True)  14.1 us
    ppermute x1, waiting for transfers between devices, with_halo(): before = lax.ppermute(last, axis, up)  10.5 us
    another operation x12, local copies, waits for them, and re-layouts  9.98 us
  transfers between devices with their start and end apart: 4, of which 4 were waited for; matrix products, arithmetic and copies ran while one was open for 1% of the time, Pallas kernels for 0%

profile of v1, /device:TPU:2, one launch (start us, length us, event | category | flops | bytes accessed | tf_op | source)
XLA Modules:
  0.0 462.4 jit_solution(18407480531897664892)
XLA Ops:
  7.2 1.8 copy.46
  9.0 1.9 collective-permute-start
  10.9 5.8 %collective-permute-start.1 = (bf16[64,2,1,4096]{3,0,2,1:T(8,128)(2,1)S(1)}, bf16[64,2,1,4096]{3,0,2,1:T(8,128)(2,1)S(1)}, u32[]{:S(2)}, u32[]{:S(2)}) collective-permute-start(bf16[64,2,1,4096]{3,0,2,1:T(8,128)(2,1)S(1)} %copy.46), channel_id=1, source_target_pairs={{1,0},{2,1},{3,2},{4,3},{5,4},{6,5},{7,6},{8,7},{9,8},{10,9},{11,1... | collective-permute-start | bytes 3145736 | tf_op jit(solution)/shard_map/ppermute | solution.py:16
  16.7 10.5 %collective-permute-done = bf16[64,2,1,4096]{3,0,2,1:T(8,128)(2,1)S(1)} collective-permute-done((bf16[64,2,1,4096]{3,0,2,1:T(8,128)(2,1)S(1)}, bf16[64,2,1,4096]{3,0,2,1:T(8,128)(2,1)S(1)}, u32[]{:S(2)}, u32[]{:S(2)}) %collective-permute-start) | collective-permute-done | bytes 1048608 | tf_op jit(solution)/shard_map/ppermute | solution.py:15
  27.2 1.8 collective-permute-done.1
  29.0 0.5 maximum_convert_fusion
  29.5 0.7 fusion.35
  30.3 1.5 select_select_fusion
  32.2 4.7 %copy.49 = bf16[64,3,1,4096]{0,1,2,3:T(4,128)(2,1)} copy(bf16[64,3,1,4096]{3,0,2,1:T(8,128)(2,1)S(1)} %pad_maximum_fusion.2) | data formatting | bytes 3145728 | tf_op jit(solution)/shard_map/stack | solution.py:36
  36.9 6.1 %reshape.243 = bf16[8,2,49152]{2,1,0:T(2,128)(2,1)S(1)} reshape(bf16[4096,1,3,64]{3,2,1,0:T(4,128)(2,1)} %bitcast.77) | data formatting | bytes 3145728
  43.0 48.1 %all_to_all.15 = bf16[8,2,49152]{2,1,0:T(2,128)(2,1)S(1)} all-to-all(bf16[8,2,49152]{2,1,0:T(2,128)(2,1)S(1)} %reshape.243), channel_id=1, replica_groups=mesh['frame'=8,'tile'=32] {'frame'}, dimensions={0} | all-to-all | bytes 3145728 | tf_op jit(solution)/shard_map/all_to_all | solution.py:55
  91.2 4.8 %reshape.244 = bf16[4096,1,3,64]{3,2,1,0:T(4,128)(2,1)} reshape(bf16[8,2,49152]{2,1,0:T(2,128)(2,1)S(1)} %all_to_all.15) | data formatting | bytes 3145728
  96.0 4.3 copy.67
  100.3 1.4 copy.51
  101.7 0.5 copy.69
  102.2 2.0 fusion.36
  104.2 0.5 all-reduce.6.cloned.1.call-start
  104.7 71.2 %all-reduce.4.cloned.1.call-done = f32[512,512]{0,1:T(8,128)} async-done(((f32[512,512]{0,1:T(8,128)}), f32[512,512]{0,1:T(8,128)}) %all-reduce.4.cloned.1.call-update) | async-done | bytes 1048592 | tf_op jit(solution)/shard_map/psum | solution.py:61
  176.2 2.1 convert_element_type.26
  178.3 0.3 copy.54
  178.6 0.8 copy.70
  179.4 112.5 %all-reduce.6.cloned.1.call-done = f32[512,512]{0,1:T(8,128)} async-done(((f32[512,512]{0,1:T(8,128)}), f32[512,512]{0,1:T(8,128)}) %all-reduce.6.cloned.1.call-update) | async-done | bytes 1048592 | tf_op jit(solution)/shard_map/psum | solution.py:61
  291.9 1.6 copy.53
  293.8 11.7 %cholesky.104 = f32[128,128]{1,0:T(8,128)S(1)} custom-call(f32[128,128]{1,0:T(8,128)S(1)} %cholesky.266), custom_call_target="Cholesky" | custom-call | tf_op jit(solution)/shard_map/jit(cholesky)/cholesky | solution.py:62
  305.7 9.8 %custom-call.30 = f32[1,128,128]{1,2,0:T(8,128)S(1)} custom-call(f32[1,128,128]{2,1,0:T(8,128)S(1)} %get-tuple-element.45), custom_call_target="InvertDiagBlocksLowerTriangular" | custom-call | tf_op jit(solution)/shard_map/jit(cholesky)/cholesky | solution.py:62
  315.5 0.3 constant_dynamic-update-slice_fusion.3
  315.9 0.3 convolution_subtract_fusion.3
  316.2 11.7 %cholesky.217 = f32[128,128]{1,0:T(8,128)S(1)} custom-call(f32[128,128]{1,0:T(8,128)S(1)} %cholesky.270), custom_call_target="Cholesky" | custom-call | tf_op jit(solution)/shard_map/jit(cholesky)/cholesky | solution.py:62
  328.0 0.6 compare_reduce_fusion.2
  328.6 0.6 compare_reduce_fusion.3
  329.2 10.0 %custom-call.31 = f32[1,128,128]{1,2,0:T(8,128)S(1)} custom-call(f32[1,128,128]{2,1,0:T(8,128)S(1)} %get-tuple-element.42), custom_call_target="InvertDiagBlocksLowerTriangular" | custom-call | tf_op jit(solution)/shard_map/jit(cholesky)/cholesky | solution.py:62
  339.4 0.4 convolution_subtract_fusion.4
  339.8 11.7 %cholesky.238 = f32[128,128]{1,0:T(8,128)S(1)} custom-call(f32[128,128]{1,0:T(8,128)S(1)} %cholesky.275), custom_call_target="Cholesky" | custom-call | tf_op jit(solution)/shard_map/jit(cholesky)/cholesky | solution.py:62
  351.6 0.7 compare_reduce_fusion.1
  352.2 9.8 %custom-call.32 = f32[1,128,128]{1,2,0:T(8,128)S(1)} custom-call(f32[1,128,128]{2,1,0:T(8,128)S(1)} %get-tuple-element.39), custom_call_target="InvertDiagBlocksLowerTriangular" | custom-call | tf_op jit(solution)/shard_map/jit(cholesky)/cholesky | solution.py:62
  362.2 0.4 convolution_subtract_fusion.5
  362.6 11.9 %cholesky.255 = f32[128,128]{1,0:T(8,128)S(1)} custom-call(f32[128,128]{1,0:T(8,128)S(1)} %convolution_subtract_fusion.5), custom_call_target="Cholesky" | custom-call | tf_op jit(solution)/shard_map/jit(cholesky)/cholesky | solution.py:62
  374.6 0.7 compare_reduce_fusion
  377.8 0.3 multiply_bitcast_fusion
  378.1 10.0 %while.1 = (s32[]{:T(128)}, f32[512,512]{1,0:T(8,128)S(1)}, s32[4,2]{0,1:T(2,128)S(1)}, f32[4,128,128]{2,1,0:T(8,128)}, s32[]{:T(128)}) while((s32[]{:T(128)}, f32[512,512]{1,0:T(8,128)S(1)}, s32[4,2]{0,1:T(2,128)S(1)}, f32[4,128,128]{2,1,0:T(8,128)}, s32[]{:T(128)}) %tuple.39), condition=%wide.while_cond, body=%wide.while_body.sunk | while | flops 2 | bytes 132705 | solution.py:64
  378.2 0.5 fusion.46
  378.7 1.9 bitcast_dynamic-update-slice_fusion.2
  380.7 0.5 fusion.46
  381.2 1.9 bitcast_dynamic-update-slice_fusion.2
  383.2 0.5 fusion.46
  383.7 1.9 bitcast_dynamic-update-slice_fusion.2
  385.7 0.5 fusion.46
  386.2 1.9 bitcast_dynamic-update-slice_fusion.2
  388.1 40.2 %custom-call.33 = f32[4,128,128]{1,2,0:T(8,128)S(1)} custom-call(f32[4,128,128]{2,1,0:T(8,128)} %get-tuple-element.9), custom_call_target="InvertDiagBlocksLowerTriangular" | custom-call | tf_op jit(solution)/shard_map/triangular_solve | solution.py:64
  428.3 1.6 fusion.26
  429.9 2.1 convolution_subtract_fusion.2
  432.0 1.7 fusion.25
  433.7 1.9 convolution_subtract_fusion
  435.7 1.7 fusion.23
  437.4 3.4 fusion.1
  440.8 1.1 copy.57
  441.9 1.2 copy.56
  443.1 1.1 copy.55
  444.2 1.4 copy.58
  445.6 1.7 convolution_bitcast_fusion
  447.6 1.4 copy.61
  449.0 2.3 copy.60
  451.3 1.3 copy.64
  452.6 2.7 fusion.7
  (39 shorter events, 2.3 us)
Async XLA Ops:
  7.2 168.8 %all-reduce.4.cloned.1.call-start = ((), (), s32[]{:S(2)}) async-start(), calls=%async_computation.1 | async-start | bytes 2097152 | tf_op jit(solution)/shard_map/psum | solution.py:61
  9.0 18.2 %collective-permute-start = (bf16[64,2,1,4096]{3,0,2,1:T(8,128)(2,1)S(1)}, bf16[64,2,1,4096]{3,0,2,1:T(8,128)(2,1)S(1)}, u32[]{:S(2)}, u32[]{:S(2)}) collective-permute-start(bf16[64,2,1,4096]{3,0,2,1:T(8,128)(2,1)S(1)} %copy.46), channel_id=1, source_target_pairs={{0,1},{1,2},{2,3},{3,4},{4,5},{5,6},{6,7},{7,8},{8,9},{9,10},{10,1... | collective-permute-start | bytes 3145736 | tf_op jit(solution)/shard_map/ppermute | solution.py:15
  10.9 18.1 %collective-permute-start.1 = (bf16[64,2,1,4096]{3,0,2,1:T(8,128)(2,1)S(1)}, bf16[64,2,1,4096]{3,0,2,1:T(8,128)(2,1)S(1)}, u32[]{:S(2)}, u32[]{:S(2)}) collective-permute-start(bf16[64,2,1,4096]{3,0,2,1:T(8,128)(2,1)S(1)} %copy.46), channel_id=1, source_target_pairs={{1,0},{2,1},{3,2},{4,3},{5,4},{6,5},{7,6},{8,7},{9,8},{10,9},{11,1... | collective-permute-start | bytes 3145736 | tf_op jit(solution)/shard_map/ppermute | solution.py:16
  104.2 187.7 %all-reduce.6.cloned.1.call-start = ((), (), s32[]{:S(2)}) async-start(), calls=%async_computation.2 | async-start | bytes 2097152 | tf_op jit(solution)/shard_map/psum | solution.py:61
  291.9 1.7 copy-start.1
  388.1 40.2 %copy-start.3 = (f32[512,512]{1,0:T(8,128)}, f32[512,512]{1,0:T(8,128)S(1)}, u32[]{:S(2)}) copy-start(f32[512,512]{1,0:T(8,128)S(1)} %get-tuple-element.101) | copy-start | bytes 3145732
  428.3 1.6 copy-start.4
  429.9 3.8 copy-start
  443.1 4.3 copy-start.2
Sparse Core Ops, SparseCore 0:
  104.3 71.5 all-reduce.3
  179.1 112.7 all-reduce.5
